TPU v7x, 128 devices: a whole 4x4x4 slice. The times are simulated.
128 devices in a mesh: list: 8 (over z, core), fsdp: 16 (over x, y).
Axes of the slice: x: 4, y: 4, z: 4, core: 2. Of those that a mesh axis runs over, the one named last changes fastest.
Arguments:
- hidden: bfloat16 [2048, 64, 2048], P(('list', 'fsdp')), may hold values from -6 to 6
- norm_gain: float32 [2048], replicated, may hold values from 0.5 to 1.5
- w_qkv: bfloat16 [2048, 1536], P('fsdp'), may hold values from -0.125 to 0.125
- w_out: bfloat16 [1024, 2048], P('fsdp'), may hold values from -0.1875 to 0.1875
- final_gain: float32 [2048], replicated, may hold values from 0.5 to 1.5
- w_score: float32 [2048], replicated, may hold values from -0.125 to 0.125
- prior: float32 [2048], P(('list', 'fsdp')), may hold values from -8 to 400
- labels: int32 [2048], P(('list', 'fsdp')), may hold values from 0 to 3
- lengths: int32 [64], replicated, may hold values from 1 to 48, 2048 in all
Outputs:
- loss: float32 [], replicated
- grad_qkv: float32 [2048, 1536], P('fsdp', 'list')
- grad_out: float32 [1024, 2048], P('fsdp', 'list')
Inputs may be any that keep to these rules, and one draw needn't show every extreme that they name: `lengths`: the longest list holds exactly 48 passages.
All inputs are finite; a program needn't handle non-finite values.
Results may differ from a plain program's by a relative error of at most 0.025.
Values may be sent and summed in bfloat16 or wider, within the bound.
A program may use at most 128 MiB of HBM per device.

v0:
```python
import jax
import jax.numpy as jnp
from jax import lax
from jax.sharding import Mesh
from jax.sharding import PartitionSpec as P

HEADS = 16
KV_HEADS = 4
HEAD_DIM = 64
PASSAGE_LEN = 64
FSDP = ("fsdp_0", "fsdp_1")
LIST_FSDP = ("list_0", "list_1", "fsdp_0", "fsdp_1")
LIST = ("list_0", "list_1")
epsilon = 1e-05
loss_scale = 64.0


def collected_together(value, axis):
    leaves = jax.tree.leaves(value)
    order = sorted(range(len(leaves)), key=lambda k: -leaves[k].size)
    width = (1, *leaves[order[0]].shape)[-1]
    lines = [
        jnp.pad(leaves[k].reshape(-1), (0, -leaves[k].size % width)).reshape(-1, width)
        for k in order
    ]
    both, at, found = (lax.all_gather(jnp.concatenate(lines), axis), 0, {})
    for k, line in zip(order, lines):
        slab = both[:, at : at + len(line)].reshape(len(both), -1)
        found[k] = slab[:, : leaves[k].size].reshape(-1, *leaves[k].shape)
        at += len(line)
    numbers = iter(range(len(leaves)))
    return jax.tree.map(lambda _: found[next(numbers)], value)


def joined_all(value, axes, combine):
    for axis in axes:
        pieces = collected_together(value, axis)
        value = jax.tree.map(lambda part: part[0], pieces)
        for k in range(1, lax.axis_size(axis)):
            value = combine(value, jax.tree.map(lambda part: part[k], pieces))
    return value


def by_axis(value, axes):
    for axis in axes:
        value = lax.psum(value, axis)
    return value


def own_rows(terms, axes):
    so_far = terms.astype(jnp.bfloat16)
    for axis in axes:
        so_far = lax.psum_scatter(so_far, axis, scatter_dimension=0, tiled=True)
    return so_far.astype(jnp.float32)


def joined_along(parts, dim):
    dims = list(parts.shape[1:])
    dims[dim] *= parts.shape[0]
    return jnp.moveaxis(parts, 0, dim).reshape(dims)


def from_everyone(value, axis):
    copies = jnp.broadcast_to(value, (lax.axis_size(axis), *value.shape))
    return lax.all_to_all(copies, axis, split_axis=0, concat_axis=0, tiled=True)


def gathered_copies(value, axis, dim):
    return joined_along(from_everyone(value, axis), dim)


def in_blocks(value, dim, count):
    dims = value.shape
    parts = value.reshape(*dims[:dim], count, dims[dim] // count, *dims[dim + 1 :])
    return jnp.moveaxis(parts, dim, 0)


def sum_packed(arrays, axis, dims):
    count = lax.axis_size(axis)
    parts = [in_blocks(a, dim, count) for a, dim in zip(arrays, dims)]
    lines = jnp.concatenate([b.reshape(count, -1) for b in parts], axis=1)
    width = max(16, -(-lines.shape[1] // 1024) * 8)
    lines = jnp.pad(lines, ((0, 0), (0, width * 128 - lines.shape[1]))).reshape(-1, 128)
    flat, at, gathered = (lax.psum_scatter(lines, axis, tiled=True).reshape(-1), 0, [])
    for b in parts:
        part = b[0]
        gathered.append(flat[at : at + part.size].reshape(part.shape))
        at += part.size
    return tuple(gathered)


def normed(hidden, norm_gain):
    values = hidden.astype(jnp.float32)
    mean_square = jnp.mean(values * values, -1, keepdims=True)
    return (values * lax.rsqrt(mean_square + epsilon) * norm_gain).astype(jnp.bfloat16)


def attend(projected, passages):
    width_q = HEADS * HEAD_DIM
    width_k = KV_HEADS * HEAD_DIM
    ratio = HEADS // KV_HEADS
    query_part = projected[:, :width_q].reshape(passages, PASSAGE_LEN, KV_HEADS, ratio, HEAD_DIM)
    key_part = projected[:, width_q : width_q + width_k].reshape(
        passages, PASSAGE_LEN, KV_HEADS, HEAD_DIM
    )
    value_part = projected[:, width_q + width_k :].reshape(
        passages, PASSAGE_LEN, KV_HEADS, HEAD_DIM
    )
    scores = jnp.einsum(
        "bqgre,bkge->bgrqk", query_part, key_part, preferred_element_type=jnp.float32
    ) * HEAD_DIM ** (-0.5)
    peak = jnp.max(scores, -1, keepdims=True)
    expo = jnp.exp(scores - peak)
    probs = (expo / jnp.sum(expo, -1, keepdims=True)).astype(jnp.bfloat16)
    attended = jnp.einsum(
        "bgrqk,bkge->bqgre", probs, value_part, preferred_element_type=jnp.float32
    ).astype(jnp.bfloat16)
    return (
        query_part,
        key_part,
        value_part,
        probs,
        attended.reshape(passages, PASSAGE_LEN, width_q),
    )


def attend_back(query_part, key_part, value_part, probs, d_attended, passages):
    d_heads = d_attended.reshape(passages, KV_HEADS, HEADS // KV_HEADS, HEAD_DIM)
    d_probs = jnp.einsum("bgre,bkge->bgrk", d_heads, value_part, preferred_element_type=jnp.float32)
    probs_f = probs.astype(jnp.float32)
    inner = jnp.sum(probs_f * d_probs[:, :, :, None, :], -1, keepdims=True)
    d_scores = (probs_f * (d_probs[:, :, :, None, :] - inner) * HEAD_DIM ** (-0.5)).astype(
        jnp.bfloat16
    )
    d_query = jnp.einsum(
        "bgrqk,bkge->bqgre", d_scores, key_part, preferred_element_type=jnp.float32
    ).astype(jnp.bfloat16)
    d_key = jnp.einsum(
        "bgrqk,bqgre->bkge", d_scores, query_part, preferred_element_type=jnp.float32
    ).astype(jnp.bfloat16)
    d_value = jnp.einsum(
        "bgrqk,bgre->bkge", probs, d_heads, preferred_element_type=jnp.float32
    ).astype(jnp.bfloat16)
    rows = passages * PASSAGE_LEN
    return jnp.concatenate(
        [d_query.reshape(rows, -1), d_key.reshape(rows, -1), d_value.reshape(rows, -1)], 1
    )


def combine_stats(first, second):
    peak = jnp.maximum(first[0], second[0])
    total = first[1] * jnp.exp(first[0] - peak) + second[1] * jnp.exp(second[0] - peak)
    return (peak, total, first[2] + second[2])


def local(hidden, norm_gain, w_qkv, w_out, final_gain, w_score, prior, labels, lengths):
    passages = hidden.shape[0]
    width = hidden.shape[2]
    normal_rows = normed(hidden, norm_gain).reshape(passages * PASSAGE_LEN, width)
    full_qkv, full_out = (
        lax.all_gather(w_qkv, FSDP, axis=0, tiled=True),
        lax.all_gather(w_out, FSDP, axis=0, tiled=True),
    )
    projected = jnp.dot(normal_rows, full_qkv, preferred_element_type=jnp.float32).astype(
        jnp.bfloat16
    )
    query_part, key_part, value_part, probs, attended = attend(projected, passages)
    mixed = jnp.dot(
        attended.reshape(passages * PASSAGE_LEN, -1), full_out, preferred_element_type=jnp.float32
    )
    residual = hidden.astype(jnp.float32) + mixed.reshape(passages, PASSAGE_LEN, width)
    pooled = jnp.mean(residual, 1)
    inverse = lax.rsqrt(jnp.mean(pooled * pooled, -1, keepdims=True) + epsilon)
    unit = pooled * inverse
    score = jnp.sum(unit * final_gain * w_score, -1) + prior
    queries = lengths.shape[0]
    position = lax.axis_index(LIST_FSDP) * passages + jnp.arange(passages, dtype=jnp.int32)
    ends = jnp.cumsum(lengths)
    owner = jnp.sum((position[:, None] >= ends[None, :]).astype(jnp.int32), 1)
    member = (owner[:, None] == jnp.arange(queries, dtype=jnp.int32)[None, :]).astype(jnp.float32)
    label_weight = jnp.exp(labels.astype(jnp.float32))
    label_local = jnp.sum(member * label_weight[:, None], 0)
    local_peak = jnp.max(jnp.where(member > 0, score[:, None], -1e30), 0)
    own_peak = jnp.sum(member * local_peak[None, :], 1)
    expo_local = jnp.sum(member * jnp.exp(score - own_peak)[:, None], 0)
    peak, total, label_total = joined_all(
        (local_peak, expo_local, label_local), LIST_FSDP, combine_stats
    )
    log_norm = peak + jnp.log(total)
    log_prob = score - jnp.sum(member * log_norm[None, :], 1)
    target = label_weight / jnp.sum(member * label_total[None, :], 1)
    loss = by_axis(-loss_scale * jnp.sum(target * log_prob), LIST_FSDP)
    d_score = loss_scale * (jnp.exp(log_prob) - target)
    d_unit = d_score[:, None] * w_score[None, :] * final_gain[None, :]
    d_pooled = inverse * (d_unit - unit * jnp.mean(d_unit * unit, -1, keepdims=True))
    d_rows = (d_pooled / PASSAGE_LEN).astype(jnp.bfloat16)
    attn_sum = jnp.sum(attended, 1, dtype=jnp.float32).astype(jnp.bfloat16)
    d_attended = lax.dot_general(
        d_rows, full_out, (((1,), (1,)), ((), ())), preferred_element_type=jnp.float32
    ).astype(jnp.bfloat16)
    d_projected = attend_back(query_part, key_part, value_part, probs, d_attended, passages)
    qkv_part = own_rows(
        lax.dot_general(
            normal_rows, d_projected, (((0,), (0,)), ((), ())), preferred_element_type=jnp.float32
        ),
        FSDP,
    )
    group_sums = lax.all_to_all(attn_sum, FSDP, split_axis=1, concat_axis=0, tiled=True)
    group_rows = gathered_copies(d_rows, FSDP, 0)
    out_part = lax.dot_general(
        group_sums, group_rows, (((0,), (0,)), ((), ())), preferred_element_type=jnp.float32
    )
    grad_qkv, grad_out = tuple(
        (
            part.astype(jnp.float32)
            for part in sum_packed(
                (qkv_part.astype(jnp.bfloat16), out_part.astype(jnp.bfloat16)), LIST, (1, 1)
            )
        )
    )
    return (loss, grad_qkv, grad_out)


def solution(mesh):
    torus = Mesh(mesh.devices.reshape(4, 2, 4, 4), ("list_0", "list_1", "fsdp_0", "fsdp_1"))
    in_specs = (
        P(LIST_FSDP, None, None),
        P(),
        P(FSDP, None),
        P(FSDP, None),
        P(),
        P(),
        P(LIST_FSDP),
        P(LIST_FSDP),
        P(),
    )
    out_specs = (P(), P(FSDP, LIST), P(FSDP, LIST))
    return jax.shard_map(local, mesh=torus, in_specs=in_specs, out_specs=out_specs, check_vma=False)
```

profile of v0, /device:TPU:0, one launch (start us, length us, event | category | flops | bytes accessed | tf_op | source)
XLA Modules:
  0.0 379.6 jit_solution(12760999220482166367)
XLA Ops:
  9.9 3.2 fusion.3
  13.1 3.0 fusion.5
  16.1 57.7 %all-gather.11.cloned.1.call-done = bf16[2048,1536]{1,0:T(8,128)(2,1)} async-done(((bf16[128,1536]{1,0:T(8,128)(2,1)}), bf16[2048,1536]{1,0:T(8,128)(2,1)}) %all-gather.11.cloned.1.call-update) | async-done | bytes 6291472 | tf_op jit(solution)/shard_map/all_gather | solution.py:161
  73.8 10.0 %convolution_convert_fusion.1 = bf16[1024,1536]{1,0:T(8,128)(2,1)S(1)} fusion(bf16[1024,2048]{1,0:T(8,128)(2,1)} %bitcast.332, bf16[2048,1536]{1,0:T(8,128)(2,1)} %all-gather.11.cloned.1.call-done), kind=kOutput, calls=%fused_computation.28 | convolution fusion | flops 6444023808 | bytes 13631488 | tf_op jit(solution)/shard_map/dot_general | solution.py:164
  85.2 2.0 reshape.843
  88.7 4.0 %reshape.844 = bf16[16,64,4,4,64]{4,3,2,1,0:T(4,128)(2,1)} reshape(bf16[1024,1024]{1,0:T(8,128)(2,1)S(1)} %slice.288) | data formatting | bytes 4194304 | tf_op jit(solution)/shard_map/reshape | solution.py:102
  92.7 8.2 %copy.67 = bf16[16,64,4,4,64]{1,4,3,2,0:T(8,128)(2,1)} copy(bf16[16,64,4,4,64]{4,3,2,1,0:T(4,128)(2,1)} %reshape.844) | data formatting | bytes 4194304 | tf_op jit(solution)/shard_map/reshape | solution.py:102
  101.3 8.6 %fusion.92 = (f32[16,4,4,64]{3,2,1,0:T(4,128)S(1)}, f32[16,4,4,64,64]{3,4,2,1,0:T(8,128)}) fusion(bf16[16,64,4,64,1]{1,3,4,2,0:T(8,128)(2,1)S(1)} %copy-done.3, bf16[16,64,4,4,64]{1,4,3,2,0:T(8,128)(2,1)} %copy.67), kind=kOutput, calls=%fused_computation.172 | convolution fusion | flops 137363520 | bytes 6881280 | tf_op jit(solution)/shard_map/sub | solution.py:113
  109.9 5.7 %convert_reduce_fusion = (bf16[16,4,4,64]{3,2,1,0:T(4,128)(2,1)S(1)}, bf16[16,4,4,64,64]{3,4,2,1,0:T(8,128)(2,1)S(1)}) fusion(f32[16,4,4,64,64]{3,4,2,1,0:T(8,128)} %get-tuple-element.31, f32[16,4,4,64]{3,2,1,0:T(4,128)S(1)} %get-tuple-element.30), kind=kLoop, calls=%fused_computation.2 | loop fusion | flops 4177920 | bytes 6389760 | tf_op jit(solution)/shard_map/bgrqk,bgre->bkge/reduce_sum | solution.py:141
  115.7 2.1 fusion.93
  117.8 5.4 %copy.62 = bf16[16,64,4,4,64]{4,3,2,1,0:T(4,128)(2,1)} copy(bf16[16,64,4,4,64]{4,1,3,2,0:T(8,128)(2,1)S(1)} %get-tuple-element.33) | data formatting | bytes 4194304 | tf_op jit(solution)/shard_map/convert_element_type | solution.py:117
  123.3 7.9 %dot_general.38 = bf16[16,64,1024]{2,1,0:T(8,128)(2,1)} reshape(bf16[16,64,4,4,64]{4,3,2,1,0:T(4,128)(2,1)} %copy.62) | data formatting | bytes 4194304 | tf_op jit(solution)/shard_map/dot_general | solution.py:168
  131.2 8.7 %fusion.6 = f32[16,2048]{1,0:T(8,128)S(1)} fusion(bf16[16,64,2048]{2,1,0:T(8,128)(2,1)} %param.9, bf16[16,64,1024]{2,1,0:T(8,128)(2,1)} %dot_general.38, bf16[1024,2048]{1,0:T(8,128)(2,1)} %all-gather.13.cloned.1.call-done), kind=kOutput, calls=%fused_computation.12 | convolution fusion | flops 4301225984 | bytes 10616832 | tf_op jit(solution)/shard_map/dot_general | solution.py:168
  140.7 11.3 %all-gather.4 = f32[4,3,64]{2,1,0:T(4,128)S(1)} all-gather(f32[1,3,64]{2,1,0:T(4,128)S(1)} %maximum_bitcast_fusion), channel_id=2, replica_groups=mesh['list_0'=4,'list_1'=2,'fsdp_0'=4,'fsdp_1'=4] {'list_0'}, dimensions={0}, use_global_device_ids=true | all-gather | bytes 3840 | tf_op jit(solution)/shard_map/all_gather | solution.py:26
  152.0 1.8 all-gather.5
  153.9 11.1 %all-gather.6 = f32[4,3,64]{2,1,0:T(4,128)S(1)} all-gather(f32[1,3,64]{2,1,0:T(4,128)S(1)} %maximum_bitcast_fusion.2), channel_id=4, replica_groups=mesh['list_0'=4,'list_1'=2,'fsdp_0'=4,'fsdp_1'=4] {'fsdp_0'}, dimensions={0}, use_global_device_ids=true | all-gather | bytes 3840 | tf_op jit(solution)/shard_map/all_gather | solution.py:26
  165.1 10.5 %all-gather.7 = f32[4,3,64]{2,1,0:T(4,128)S(1)} all-gather(f32[1,3,64]{2,1,0:T(4,128)S(1)} %maximum_bitcast_fusion.3), channel_id=5, replica_groups=mesh['list_0'=4,'list_1'=2,'fsdp_0'=4,'fsdp_1'=4] {'fsdp_1'}, dimensions={0}, use_global_device_ids=true | all-gather | bytes 3840 | tf_op jit(solution)/shard_map/all_gather | solution.py:26
  178.1 9.1 %convert_bitcast_fusion = bf16[16,64,4,4,64]{1,4,3,2,0:T(8,128)(2,1)} fusion(bf16[16,64,4,64,1]{1,3,4,2,0:T(8,128)(2,1)S(1)} %copy-done.3, bf16[16,4,4,64,64]{3,4,2,1,0:T(8,128)(2,1)} %copy-done, f32[16,4,4,64]{3,2,1,0:T(4,128)S(1)} %fusion.31), kind=kOutput, calls=%fused_computation.24 | convolution fusion | flops 142622784 | bytes 4784128 | tf_op jit(solution)/shard_map/bgrqk,bkge->bqgre/dot_general | solution.py:135
  187.1 10.4 %fusion.28 = bf16[16,64,4,64]{1,3,2,0:T(8,128)(2,1)} fusion(bf16[16,64,4,4,64]{1,4,3,2,0:T(8,128)(2,1)} %copy.67, bf16[16,4,4,64,64]{3,4,2,1,0:T(8,128)(2,1)} %copy-done, f32[16,4,4,64]{3,2,1,0:T(4,128)S(1)} %fusion.31), kind=kOutput, calls=%fused_computation.40 | convolution fusion | flops 141836352 | bytes 4784128 | tf_op jit(solution)/shard_map/bgrqk,bqgre->bkge/dot_general | solution.py:138
  197.5 7.6 %copy.66 = bf16[16,64,4,4,64]{1,0,4,3,2:T(8,128)(2,1)} copy(bf16[16,64,4,4,64]{1,4,3,2,0:T(8,128)(2,1)} %convert_bitcast_fusion) | data formatting | bytes 4194304 | tf_op jit(solution)/shard_map/convert_element_type | solution.py:137
  205.2 5.5 %reshape.849 = bf16[1024,1024]{0,1:T(8,128)(2,1)S(1)} reshape(bf16[16,64,4,4,64]{1,0,4,3,2:T(8,128)(2,1)} %copy.66) | data formatting | bytes 4194304 | tf_op jit(solution)/shard_map/reshape | solution.py:146
  210.6 1.9 copy.69
  216.8 11.7 %convolution_convert_fusion = bf16[2048,1536]{1,0:T(8,128)(2,1)} fusion(bf16[1024,2048]{1,0:T(8,128)(2,1)} %bitcast.333, bf16[1024,256]{0,1:T(8,128)(2,1)} %reshape.851, bf16[1024,256]{0,1:T(8,128)(2,1)} %reshape.850, bf16[1024,1024]{0,1:T(8,128)(2,1)S(1)} %reshape.849), kind=kOutput, calls=%fused_computation.20 | convolution fusion | flops 6455033856 | bytes 13631488 | tf_op jit(solution)/shard_map/dot_general | solution.py:203
  228.6 62.7 %reduce-scatter.4.cloned.1.call-done = bf16[512,1536]{1,0:T(8,128)(2,1)} async-done(((bf16[2048,1536]{1,0:T(8,128)(2,1)}), bf16[512,1536]{1,0:T(8,128)(2,1)}) %reduce-scatter.4.cloned.1.call-update) | async-done | bytes 1572880 | tf_op jit(solution)/shard_map/reduce_scatter | solution.py:53
  291.5 12.7 %all_to_all.21 = bf16[16,2,512]{2,1,0:T(2,128)(2,1)S(1)} all-to-all(bf16[16,2,512]{2,1,0:T(2,128)(2,1)S(1)} %reshape.882), channel_id=1, replica_groups=mesh['list_0'=4,'list_1'=2,'fsdp_0'=4,'fsdp_1'=4] {'fsdp_0','fsdp_1'}, dimensions={0} | all-to-all | bytes 65536 | tf_op jit(solution)/shard_map/all_to_all | solution.py:208
  305.3 3.7 all-to-all-start.1
  309.1 16.2 %all-to-all-done.1 = bf16[16,16,2048]{2,1,0:T(8,128)(2,1)S(1)} async-done(((bf16[16,16,2048]{2,1,0:T(8,128)(2,1)}), bf16[16,16,2048]{2,1,0:T(8,128)(2,1)S(1)}, u32[]{:S(2)}, u32[]{:S(2)}) %all-to-all-start.1) | async-done | bytes 1048608 | tf_op jit(solution)/shard_map/all_to_all | solution.py:65
  325.7 4.3 %reduce-scatter.6.cloned.1.call-done = bf16[128,1536]{1,0:T(8,128)(2,1)} async-done(((bf16[512,1536]{1,0:T(8,128)(2,1)}), bf16[128,1536]{1,0:T(8,128)(2,1)}) %reduce-scatter.6.cloned.1.call-update) | async-done | bytes 393232 | tf_op jit(solution)/shard_map/reduce_scatter | solution.py:53
  334.5 11.2 %psum.28 = f32[]{:T(128)} all-reduce(f32[]{:T(128)S(6)} %mul_shard_map.3), channel_id=1, replica_groups=mesh['list_0'=4,'list_1'=2,'fsdp_0'=4,'fsdp_1'=4] {'list_0'}, use_global_device_ids=true, to_apply=%region_15.16 | all-reduce | flops 1 | bytes 8 | tf_op jit(solution)/shard_map/psum | solution.py:46
  345.7 3.1 psum.29
  348.7 11.3 %psum.30 = f32[]{:T(128)} all-reduce(f32[]{:T(128)} %psum.29), channel_id=1, replica_groups=mesh['list_0'=4,'list_1'=2,'fsdp_0'=4,'fsdp_1'=4] {'fsdp_0'}, use_global_device_ids=true, to_apply=%region_17.18 | all-reduce | flops 1 | bytes 8 | tf_op jit(solution)/shard_map/psum | solution.py:46
  360.0 9.8 %psum.31 = f32[]{:T(128)} all-reduce(f32[]{:T(128)} %psum.30), channel_id=1, replica_groups=mesh['list_0'=4,'list_1'=2,'fsdp_0'=4,'fsdp_1'=4] {'fsdp_1'}, use_global_device_ids=true, to_apply=%region_18.19 | all-reduce | flops 1 | bytes 8 | tf_op jit(solution)/shard_map/psum | solution.py:46
  (91 shorter events, 22.1 us)
Async XLA Ops:
  7.2 5.9 %copy-start.7 = (f32[2048]{0:T(1024)S(1)}, f32[2048]{0:T(1024)}, u32[]{:S(2)}) copy-start(f32[2048]{0:T(1024)} %param.10) | copy-start | bytes 24580
  7.2 66.7 %all-gather.11.cloned.1.call-start = ((), (), s32[]{:S(2)}) async-start(), calls=%async_computation.5 | async-start | bytes 6684672 | tf_op jit(solution)/shard_map/all_gather | solution.py:161
  7.9 123.3 %all-gather.13.cloned.1.call-start = ((), (), s32[]{:S(2)}) async-start(), calls=%async_computation.6 | async-start | bytes 4456448 | tf_op jit(solution)/shard_map/all_gather | solution.py:162
  8.7 282.6 %reduce-scatter.4.cloned.1.call-start = ((), (), s32[]{:S(2)}) async-start(), calls=%async_computation.7 | async-start | bytes 7864320 | tf_op jit(solution)/shard_map/reduce_scatter | solution.py:53
  9.7 3.5 copy-start.1
  92.7 8.2 %copy-start.4 = (bf16[1024,256]{1,0:T(8,128)(2,1)S(1)}, bf16[1024,256]{1,0:T(8,128)(2,1)}, u32[]{:S(2)}) copy-start(bf16[1024,256]{1,0:T(8,128)(2,1)} %get-tuple-element.26) | copy-start | bytes 1572868
  92.7 8.7 %copy-start.3 = (bf16[16,64,4,64,1]{1,3,4,2,0:T(8,128)(2,1)S(1)}, bf16[16,64,4,64,1]{1,3,4,2,0:T(8,128)(2,1)}, u32[]{:S(2)}) copy-start(bf16[16,64,4,64,1]{1,3,4,2,0:T(8,128)(2,1)} %copy.78) | copy-start | bytes 1572868
  115.7 2.2 copy-start
  131.1 8.9 %copy-start.5 = (f32[2048]{0:T(1024)S(1)}, f32[2048]{0:T(1024)}, u32[]{:S(2)}) copy-start(f32[2048]{0:T(1024)} %param.14) | copy-start | bytes 24580
  131.1 8.9 %copy-start.6 = (f32[2048]{0:T(1024)S(1)}, f32[2048]{0:T(1024)}, u32[]{:S(2)}) copy-start(f32[2048]{0:T(1024)} %param.13) | copy-start | bytes 24580
  131.1 9.1 %copy-start.9 = (f32[16]{0:T(128)S(1)}, f32[16]{0:T(128)}, u32[]{:S(2)}) copy-start(f32[16]{0:T(128)} %param.15) | copy-start | bytes 196
  131.1 9.4 %copy-start.8 = (s32[16]{0:T(128)S(1)}, s32[16]{0:T(128)}, u32[]{:S(2)}) copy-start(s32[16]{0:T(128)} %param.16) | copy-start | bytes 196
  131.2 44.9 %copy-start.2 = (bf16[1024,2048]{1,0:T(8,128)(2,1)S(1)}, bf16[1024,2048]{1,0:T(8,128)(2,1)}, u32[]{:S(2)}) copy-start(bf16[1024,2048]{1,0:T(8,128)(2,1)} %all-gather.13.cloned.1.call-done) | copy-start | bytes 12582916
  228.5 101.5 %reduce-scatter.6.cloned.1.call-start = ((), (), s32[]{:S(2)}) async-start(), calls=%async_computation.8 | async-start | bytes 1966080 | tf_op jit(solution)/shard_map/reduce_scatter | solution.py:53
  305.3 20.1 %all-to-all-start.1 = ((bf16[16,16,2048]{2,1,0:T(8,128)(2,1)}), bf16[16,16,2048]{2,1,0:T(8,128)(2,1)S(1)}, u32[]{:S(2)}, u32[]{:S(2)}) async-start(bf16[16,16,2048]{2,1,0:T(8,128)(2,1)} %broadcast_in_dim.12), calls=%async_computation.3 | async-start | bytes 2097152 | tf_op jit(solution)/shard_map/all_to_all | solution.py:65
  308.9 60.9 %reduce-scatter.8.cloned.1.call-start = ((), (), s32[]{:S(2)}) async-start(), calls=%async_computation.9 | async-start | bytes 737280 | tf_op jit(solution)/shard_map/reduce_scatter | solution.py:84
Sparse Core Ops, SparseCore 0:
  10.2 63.6 all-gather.10
  76.0 50.9 all-gather.12
  228.7 62.6 reduce-scatter.3
  293.6 36.3 reduce-scatter.5
  333.3 31.6 reduce-scatter.7
where the time goes:
time: 386 us; the launch traced here: 380 us
  waiting for transfers between devices  142 us (37%)
  blocking collectives  82.7 us (21%)
  matrix products  63.3 us (16%)
  local copies, waits for them, and re-layouts  56.4 us (15%)
  other arithmetic  15.9 us (4%)
  between operations  15 us (4%)
    reduce_scatter x2, waiting for transfers between devices, own_rows(): so_far = lax.psum_scatter(so_far, axis, scatter_dimension=0, tiled=True)  67 us
    all_gather x1, waiting for transfers between devices, local(): lax.all_gather(w_qkv, FSDP, axis=0, tiled=True)  57.7 us
    psum x4, blocking collectives, by_axis(): value = lax.psum(value, axis)  35.3 us
    all_gather x4, blocking collectives, collected_together(): both, at, found = (lax.all_gather(jnp.concatenate(lines), axis), 0, {})  34.7 us
    all_to_all x1, waiting for transfers between devices, from_everyone(): return lax.all_to_all(copies, axis, split_axis=0, concat_axis=0, tiled=True)  16.2 us
    all_to_all x1, blocking collectives, local(): lax.all_to_all(attn_sum, FSDP, split_axis=1, concat_axis=0, tiled=True)  12.7 us
    reshape x2, local copies, waits for them, and re-layouts, attend(): projected[:, :width_q]  12.2 us
    dot_general x1, matrix products, local(): lax.dot_general(normal_rows, d_projected, (((0,), (0,)), ((), ())), prefe...  11.7 us
  transfers between devices with their start and end apart: 6, of which 4 were waited for; matrix products, arithmetic and copies ran while one was open for 18% of the time, Pallas kernels for 0%

commit v1 on v0

--- a/solution.py
+++ b/solution.py
@@ -13,6 +13,13 @@
 LIST = ("list_0", "list_1")
 epsilon = 1e-05
 loss_scale = 64.0
+
+
+def gather_over(value, mesh_axis, dim):
+    size = lax.axis_size(mesh_axis)
+    tiles = jnp.stack([value for _ in range(size)])
+    tiles = lax.all_to_all(tiles, mesh_axis, split_axis=0, concat_axis=0)
+    return jnp.concatenate(tiles, axis=dim)
 
 
 def collected_together(value, axis):
@@ -158,7 +165,7 @@
     width = hidden.shape[2]
     normal_rows = normed(hidden, norm_gain).reshape(passages * PASSAGE_LEN, width)
     full_qkv, full_out = (
-        lax.all_gather(w_qkv, FSDP, axis=0, tiled=True),
+        gather_over(w_qkv, FSDP, 0),
         lax.all_gather(w_out, FSDP, axis=0, tiled=True),
     )
     projected = jnp.dot(normal_rows, full_qkv, preferred_element_type=jnp.float32).astype(

time: 386 us -> 446 us (1.16)
  waiting for transfers between devices: 142 us -> 182 us
  blocking collectives: 82.7 us -> 92.3 us
  starting transfers between devices: 3.85 us -> 11.1 us
    all_to_all x0 -> x1, waiting for transfers between devices: none -> 97.3 us  [gather_over(): tiles = lax.all_to_all(tiles, mesh_axis, split_axis=0, concat_axis=0)]
    all_gather x1 -> x0, waiting for transfers between devices: 57.7 us -> none  [local(): lax.all_gather(w_qkv, FSDP, axis=0, tiled=True)]
    all_gather x4, blocking collectives: 34.7 us -> 44.2 us  [collected_together(): both, at, found = (lax.all_gather(jnp.concatenate(lines), axis), 0, {})]
    all_to_all x0 -> x1, starting transfers between devices: none -> 7.32 us  [gather_over(): tiles = lax.all_to_all(tiles, mesh_axis, split_axis=0, concat_axis=0)]
  transfers between devices with their start and end apart: 6 -> 6, of which waited for: 4 -> 4; matrix products, arithmetic and copies ran while one was open for 18% -> 15% of each run, Pallas kernels for 0% -> 0%
where the time goes in v1:
time: 446 us; the launch traced here: 439 us
  waiting for transfers between devices  182 us (41%)
  blocking collectives  92.3 us (21%)
  matrix products  63.1 us (14%)
  local copies, waits for them, and re-layouts  60 us (13%)
  other arithmetic  15.9 us (4%)
  between operations  15 us (3%)
  starting transfers between devices  11.1 us (2%)
    all_to_all x1, waiting for transfers between devices, gather_over(): tiles = lax.all_to_all(tiles, mesh_axis, split_axis=0, concat_axis=0)  97.3 us
    reduce_scatter x2, waiting for transfers between devices, own_rows(): so_far = lax.psum_scatter(so_far, axis, scatter_dimension=0, tiled=True)  67.1 us
    all_gather x4, blocking collectives, collected_together(): both, at, found = (lax.all_gather(jnp.concatenate(lines), axis), 0, {})  44.2 us
    psum x4, blocking collectives, by_axis(): value = lax.psum(value, axis)  35.3 us
    all_to_all x1, waiting for transfers between devices, from_everyone(): return lax.all_to_all(copies, axis, split_axis=0, concat_axis=0, tiled=True)  16.3 us
    all_to_all x1, blocking collectives, local(): lax.all_to_all(attn_sum, FSDP, split_axis=1, concat_axis=0, tiled=True)  12.7 us
    reshape x2, local copies, waits for them, and re-layouts, attend(): projected[:, :width_q]  12.3 us
    dot_general x1, matrix products, local(): lax.dot_general(normal_rows, d_projected, (((0,), (0,)), ((), ())), prefe...  11.7 us
  transfers between devices with their start and end apart: 6, of which 4 were waited for; matrix products, arithmetic and copies ran while one was open for 15% of the time, Pallas kernels for 0%

profile of v1, /device:TPU:0, one launch (start us, length us, event | category | flops | bytes accessed | tf_op | source)
XLA Modules:
  0.0 438.9 jit_solution(8618489066705550520)
XLA Ops:
  7.2 4.3 stack.2
  11.4 7.3 %all-to-all-start = ((bf16[16,128,1536]{2,1,0:T(8,128)(2,1)}), bf16[16,128,1536]{2,1,0:T(8,128)(2,1)}, u32[]{:S(2)}, u32[]{:S(2)}) async-start(bf16[16,128,1536]{2,1,0:T(8,128)(2,1)} %stack.2), calls=%async_computation | async-start | bytes 12582912 | tf_op jit(solution)/shard_map/all_to_all | solution.py:21
  20.1 3.2 fusion.3
  23.3 3.0 fusion.5
  26.3 97.3 %all-to-all-done = bf16[16,128,1536]{2,1,0:T(8,128)(2,1)} async-done(((bf16[16,128,1536]{2,1,0:T(8,128)(2,1)}), bf16[16,128,1536]{2,1,0:T(8,128)(2,1)}, u32[]{:S(2)}, u32[]{:S(2)}) %all-to-all-start) | async-done | bytes 6291488 | tf_op jit(solution)/shard_map/all_to_all | solution.py:21
  123.6 10.1 %convolution_convert_fusion.1 = bf16[1024,1536]{1,0:T(8,128)(2,1)S(1)} fusion(bf16[1024,2048]{1,0:T(8,128)(2,1)} %bitcast.333, bf16[2048,1536]{1,0:T(8,128)(2,1)} %bitcast.2), kind=kOutput, calls=%fused_computation.28 | convolution fusion | flops 6444023808 | bytes 13631488 | tf_op jit(solution)/shard_map/dot_general | solution.py:171
  135.1 2.0 reshape.849
  138.5 4.0 reshape.850
  142.5 8.3 %copy.67 = bf16[16,64,4,4,64]{1,4,3,2,0:T(8,128)(2,1)} copy(bf16[16,64,4,4,64]{4,3,2,1,0:T(4,128)(2,1)} %reshape.850) | data formatting | bytes 4194304 | tf_op jit(solution)/shard_map/reshape | solution.py:109
  151.2 8.6 %fusion.92 = (f32[16,4,4,64]{3,2,1,0:T(4,128)S(1)}, f32[16,4,4,64,64]{3,4,2,1,0:T(8,128)}) fusion(bf16[16,64,4,64,1]{1,3,4,2,0:T(8,128)(2,1)S(1)} %copy-done.3, bf16[16,64,4,4,64]{1,4,3,2,0:T(8,128)(2,1)} %copy.67), kind=kOutput, calls=%fused_computation.172 | convolution fusion | flops 137363520 | bytes 6881280 | tf_op jit(solution)/shard_map/sub | solution.py:120
  159.8 5.7 %convert_reduce_fusion = (bf16[16,4,4,64]{3,2,1,0:T(4,128)(2,1)S(1)}, bf16[16,4,4,64,64]{3,4,2,1,0:T(8,128)(2,1)S(1)}) fusion(f32[16,4,4,64,64]{3,4,2,1,0:T(8,128)} %get-tuple-element.31, f32[16,4,4,64]{3,2,1,0:T(4,128)S(1)} %get-tuple-element.30), kind=kLoop, calls=%fused_computation.2 | loop fusion | flops 4177920 | bytes 6389760 | tf_op jit(solution)/shard_map/bgrqk,bgre->bkge/reduce_sum | solution.py:148
  165.5 2.1 fusion.93
  167.7 5.4 %copy.62 = bf16[16,64,4,4,64]{4,3,2,1,0:T(4,128)(2,1)} copy(bf16[16,64,4,4,64]{4,1,3,2,0:T(8,128)(2,1)S(1)} %get-tuple-element.33) | data formatting | bytes 4194304 | tf_op jit(solution)/shard_map/convert_element_type | solution.py:124
  173.1 7.9 %dot_general.38 = bf16[16,64,1024]{2,1,0:T(8,128)(2,1)} reshape(bf16[16,64,4,4,64]{4,3,2,1,0:T(4,128)(2,1)} %copy.62) | data formatting | bytes 4194304 | tf_op jit(solution)/shard_map/dot_general | solution.py:175
  181.0 8.7 %fusion.6 = f32[16,2048]{1,0:T(8,128)S(1)} fusion(bf16[16,64,2048]{2,1,0:T(8,128)(2,1)} %param.9, bf16[16,64,1024]{2,1,0:T(8,128)(2,1)} %dot_general.38, bf16[1024,2048]{1,0:T(8,128)(2,1)} %all-gather.10.cloned.1.call-done), kind=kOutput, calls=%fused_computation.12 | convolution fusion | flops 4301225984 | bytes 10616832 | tf_op jit(solution)/shard_map/dot_general | solution.py:175
  190.5 15.0 %all-gather.4 = f32[4,3,64]{2,1,0:T(4,128)S(1)} all-gather(f32[1,3,64]{2,1,0:T(4,128)S(1)} %maximum_bitcast_fusion), channel_id=2, replica_groups=mesh['list_0'=4,'list_1'=2,'fsdp_0'=4,'fsdp_1'=4] {'list_0'}, dimensions={0}, use_global_device_ids=true | all-gather | bytes 3840 | tf_op jit(solution)/shard_map/all_gather | solution.py:33
  207.4 12.8 %all-gather.6 = f32[4,3,64]{2,1,0:T(4,128)S(1)} all-gather(f32[1,3,64]{2,1,0:T(4,128)S(1)} %maximum_bitcast_fusion.2), channel_id=4, replica_groups=mesh['list_0'=4,'list_1'=2,'fsdp_0'=4,'fsdp_1'=4] {'fsdp_0'}, dimensions={0}, use_global_device_ids=true | all-gather | bytes 3840 | tf_op jit(solution)/shard_map/all_gather | solution.py:33
  220.3 14.6 %all-gather.7 = f32[4,3,64]{2,1,0:T(4,128)S(1)} all-gather(f32[1,3,64]{2,1,0:T(4,128)S(1)} %maximum_bitcast_fusion.3), channel_id=5, replica_groups=mesh['list_0'=4,'list_1'=2,'fsdp_0'=4,'fsdp_1'=4] {'fsdp_1'}, dimensions={0}, use_global_device_ids=true | all-gather | bytes 3840 | tf_op jit(solution)/shard_map/all_gather | solution.py:33
  237.4 9.1 %convert_bitcast_fusion = bf16[16,64,4,4,64]{1,4,3,2,0:T(8,128)(2,1)} fusion(bf16[16,64,4,64,1]{1,3,4,2,0:T(8,128)(2,1)S(1)} %copy-done.3, bf16[16,4,4,64,64]{3,4,2,1,0:T(8,128)(2,1)} %copy-done, f32[16,4,4,64]{3,2,1,0:T(4,128)S(1)} %fusion.31), kind=kOutput, calls=%fused_computation.24 | convolution fusion | flops 142622784 | bytes 4784128 | tf_op jit(solution)/shard_map/bgrqk,bkge->bqgre/dot_general | solution.py:142
  246.5 10.1 %fusion.28 = bf16[16,64,4,64]{1,3,2,0:T(8,128)(2,1)} fusion(bf16[16,64,4,4,64]{1,4,3,2,0:T(8,128)(2,1)} %copy.67, bf16[16,4,4,64,64]{3,4,2,1,0:T(8,128)(2,1)} %copy-done, f32[16,4,4,64]{3,2,1,0:T(4,128)S(1)} %fusion.31), kind=kOutput, calls=%fused_computation.40 | convolution fusion | flops 141836352 | bytes 4784128 | tf_op jit(solution)/shard_map/bgrqk,bqgre->bkge/dot_general | solution.py:145
  256.6 7.6 %copy.66 = bf16[16,64,4,4,64]{1,0,4,3,2:T(8,128)(2,1)} copy(bf16[16,64,4,4,64]{1,4,3,2,0:T(8,128)(2,1)} %convert_bitcast_fusion) | data formatting | bytes 4194304 | tf_op jit(solution)/shard_map/convert_element_type | solution.py:144
  264.2 5.5 %reshape.855 = bf16[1024,1024]{0,1:T(8,128)(2,1)S(1)} reshape(bf16[16,64,4,4,64]{1,0,4,3,2:T(8,128)(2,1)} %copy.66) | data formatting | bytes 4194304 | tf_op jit(solution)/shard_map/reshape | solution.py:153
  275.9 11.7 %convolution_convert_fusion = bf16[2048,1536]{1,0:T(8,128)(2,1)} fusion(bf16[1024,2048]{1,0:T(8,128)(2,1)} %bitcast.334, bf16[1024,256]{0,1:T(8,128)(2,1)} %reshape.857, bf16[1024,256]{0,1:T(8,128)(2,1)} %reshape.856, bf16[1024,1024]{0,1:T(8,128)(2,1)S(1)} %reshape.855), kind=kOutput, calls=%fused_computation.20 | convolution fusion | flops 6455033856 | bytes 13631488 | tf_op jit(solution)/shard_map/dot_general | solution.py:210
  287.7 62.8 %reduce-scatter.4.cloned.1.call-done = bf16[512,1536]{1,0:T(8,128)(2,1)} async-done(((bf16[2048,1536]{1,0:T(8,128)(2,1)}), bf16[512,1536]{1,0:T(8,128)(2,1)}) %reduce-scatter.4.cloned.1.call-update) | async-done | bytes 1572880 | tf_op jit(solution)/shard_map/reduce_scatter | solution.py:60
  350.6 12.7 %all_to_all.26 = bf16[16,2,512]{2,1,0:T(2,128)(2,1)S(1)} all-to-all(bf16[16,2,512]{2,1,0:T(2,128)(2,1)S(1)} %reshape.888), channel_id=1, replica_groups=mesh['list_0'=4,'list_1'=2,'fsdp_0'=4,'fsdp_1'=4] {'fsdp_0','fsdp_1'}, dimensions={0} | all-to-all | bytes 65536 | tf_op jit(solution)/shard_map/all_to_all | solution.py:215
  364.4 3.7 all-to-all-start.2
  368.2 16.3 %all-to-all-done.2 = bf16[16,16,2048]{2,1,0:T(8,128)(2,1)S(1)} async-done(((bf16[16,16,2048]{2,1,0:T(8,128)(2,1)}), bf16[16,16,2048]{2,1,0:T(8,128)(2,1)S(1)}, u32[]{:S(2)}, u32[]{:S(2)}) %all-to-all-start.2) | async-done | bytes 1048608 | tf_op jit(solution)/shard_map/all_to_all | solution.py:72
  385.0 4.3 reduce-scatter.6.cloned.1.call-done
  393.8 11.2 %psum.28 = f32[]{:T(128)} all-reduce(f32[]{:T(128)S(6)} %mul_shard_map.3), channel_id=1, replica_groups=mesh['list_0'=4,'list_1'=2,'fsdp_0'=4,'fsdp_1'=4] {'list_0'}, use_global_device_ids=true, to_apply=%region_15.16 | all-reduce | flops 1 | bytes 8 | tf_op jit(solution)/shard_map/psum | solution.py:53
  405.0 3.1 psum.29
  408.1 11.3 %psum.30 = f32[]{:T(128)} all-reduce(f32[]{:T(128)} %psum.29), channel_id=1, replica_groups=mesh['list_0'=4,'list_1'=2,'fsdp_0'=4,'fsdp_1'=4] {'fsdp_0'}, use_global_device_ids=true, to_apply=%region_17.18 | all-reduce | flops 1 | bytes 8 | tf_op jit(solution)/shard_map/psum | solution.py:53
  419.3 9.8 %psum.31 = f32[]{:T(128)} all-reduce(f32[]{:T(128)} %psum.30), channel_id=1, replica_groups=mesh['list_0'=4,'list_1'=2,'fsdp_0'=4,'fsdp_1'=4] {'fsdp_1'}, use_global_device_ids=true, to_apply=%region_18.19 | all-reduce | flops 1 | bytes 8 | tf_op jit(solution)/shard_map/psum | solution.py:53
  (93 shorter events, 24.4 us)
Async XLA Ops:
  11.4 8.1 %copy-start.9 = (s32[64]{0:T(128)S(1)}, s32[64]{0:T(128)}, u32[]{:S(2)}) copy-start(s32[64]{0:T(128)} %param.17) | copy-start | bytes 772
  11.4 112.2 %all-to-all-start = ((bf16[16,128,1536]{2,1,0:T(8,128)(2,1)}), bf16[16,128,1536]{2,1,0:T(8,128)(2,1)}, u32[]{:S(2)}, u32[]{:S(2)}) async-start(bf16[16,128,1536]{2,1,0:T(8,128)(2,1)} %stack.2), calls=%async_computation | async-start | bytes 12582912 | tf_op jit(solution)/shard_map/all_to_all | solution.py:21
  18.8 4.6 %copy-start.7 = (f32[2048]{0:T(1024)S(1)}, f32[2048]{0:T(1024)}, u32[]{:S(2)}) copy-start(f32[2048]{0:T(1024)} %param.10) | copy-start | bytes 24580
  18.8 162.2 %all-gather.10.cloned.1.call-start = ((), (), s32[]{:S(2)}) async-start(), calls=%async_computation.6 | async-start | bytes 4456448 | tf_op jit(solution)/shard_map/all_gather | solution.py:169
  19.5 330.9 %reduce-scatter.4.cloned.1.call-start = ((), (), s32[]{:S(2)}) async-start(), calls=%async_computation.7 | async-start | bytes 7864320 | tf_op jit(solution)/shard_map/reduce_scatter | solution.py:60
  19.9 3.5 copy-start.1
  142.5 8.3 %copy-start.4 = (bf16[1024,256]{1,0:T(8,128)(2,1)S(1)}, bf16[1024,256]{1,0:T(8,128)(2,1)}, u32[]{:S(2)}) copy-start(bf16[1024,256]{1,0:T(8,128)(2,1)} %get-tuple-element.26) | copy-start | bytes 1572868
  142.5 8.7 %copy-start.3 = (bf16[16,64,4,64,1]{1,3,4,2,0:T(8,128)(2,1)S(1)}, bf16[16,64,4,64,1]{1,3,4,2,0:T(8,128)(2,1)}, u32[]{:S(2)}) copy-start(bf16[16,64,4,64,1]{1,3,4,2,0:T(8,128)(2,1)} %copy.78) | copy-start | bytes 1572868
  165.5 2.2 copy-start
  181.0 8.9 %copy-start.5 = (f32[2048]{0:T(1024)S(1)}, f32[2048]{0:T(1024)}, u32[]{:S(2)}) copy-start(f32[2048]{0:T(1024)} %param.14) | copy-start | bytes 24580
  181.0 8.9 %copy-start.6 = (f32[2048]{0:T(1024)S(1)}, f32[2048]{0:T(1024)}, u32[]{:S(2)}) copy-start(f32[2048]{0:T(1024)} %param.13) | copy-start | bytes 24580
  181.0 9.1 %copy-start.10 = (f32[16]{0:T(128)S(1)}, f32[16]{0:T(128)}, u32[]{:S(2)}) copy-start(f32[16]{0:T(128)} %param.15) | copy-start | bytes 196
  181.0 9.4 %copy-start.8 = (s32[16]{0:T(128)S(1)}, s32[16]{0:T(128)}, u32[]{:S(2)}) copy-start(s32[16]{0:T(128)} %param.16) | copy-start | bytes 196
  181.0 54.5 %copy-start.2 = (bf16[1024,2048]{1,0:T(8,128)(2,1)S(1)}, bf16[1024,2048]{1,0:T(8,128)(2,1)}, u32[]{:S(2)}) copy-start(bf16[1024,2048]{1,0:T(8,128)(2,1)} %all-gather.10.cloned.1.call-done) | copy-start | bytes 12582916
  287.6 101.7 %reduce-scatter.6.cloned.1.call-start = ((), (), s32[]{:S(2)}) async-start(), calls=%async_computation.8 | async-start | bytes 1966080 | tf_op jit(solution)/shard_map/reduce_scatter | solution.py:60
  364.4 20.2 %all-to-all-start.2 = ((bf16[16,16,2048]{2,1,0:T(8,128)(2,1)}), bf16[16,16,2048]{2,1,0:T(8,128)(2,1)S(1)}, u32[]{:S(2)}, u32[]{:S(2)}) async-start(bf16[16,16,2048]{2,1,0:T(8,128)(2,1)} %broadcast_in_dim.12), calls=%async_computation.4 | async-start | bytes 2097152 | tf_op jit(solution)/shard_map/all_to_all | solution.py:72
  368.1 61.0 %reduce-scatter.8.cloned.1.call-start = ((), (), s32[]{:S(2)}) async-start(), calls=%async_computation.9 | async-start | bytes 737280 | tf_op jit(solution)/shard_map/reduce_scatter | solution.py:91
Sparse Core Ops, SparseCore 0:
  21.7 119.7 all-gather.9
  287.7 62.6 reduce-scatter.3
  352.9 36.3 reduce-scatter.5
  392.6 31.6 reduce-scatter.7
